TPU v7x, 32 devices: a whole 2x2x4 slice. The times are simulated.
32 devices in a mesh: tiles: 2 (over x), space: 8 (over z, y), chan: 2 (over core).
Axes of the slice: x: 2, y: 2, z: 4, core: 2. Of those that a mesh axis runs over, the one named last changes fastest.
Arguments:
- volume: bfloat16 [32, 64, 32, 256], P(None, 'space', 'tiles', 'chan'), parts along dimension 2, may hold values from -6 to 6
- weight_one: bfloat16 [3, 3, 3, 256, 256], replicated, may hold values from -0.078125 to 0.078125
- bias_one: float32 [256], replicated, may hold values from -3 to 3
- weight_two: bfloat16 [3, 3, 3, 256, 256], replicated, may hold values from -0.078125 to 0.078125
- bias_two: float32 [256], replicated, may hold values from -3 to 3
Outputs:
- features: bfloat16 [32, 64, 32, 256], P('space', None, 'tiles', 'chan'), parts along dimension 2
There are 2 independent parts, one for each index of `tiles`. A program takes and returns all parts, laid end to end along the dimension named above; an argument that names none is the same for every part. Nothing has to cross between parts.
All inputs are finite; a program needn't handle non-finite values.
Results may differ from a plain program's by a relative error of at most 0.0044.
Values may be sent and summed in bfloat16 or wider, within the bound.
A program may use at most 128 MiB of HBM per device.

v0:
```python
import jax
import jax.numpy as jnp
from jax import lax
from jax.sharding import PartitionSpec as P


def padded(x, sides, width):
    for axis, dim in sides:
        devices, length = (lax.axis_size(axis), x.shape[dim])
        up = [(i, (i + 1) % devices) for i in range(devices - 1)]
        down = [(j, i) for i, j in up]
        last = lax.slice_in_dim(x, length - width, length, axis=dim)
        first = lax.slice_in_dim(x, 0, width, axis=dim)
        before = lax.ppermute(last, axis, up)
        after = lax.ppermute(first, axis, down)
        x = jnp.concatenate([before, x, after], axis=dim)
    return x


def convolve(field, kernel):
    return lax.conv_general_dilated(
        field[None],
        kernel,
        (1, 1, 1),
        ((0, 0), (1, 1), (1, 1)),
        dimension_numbers=("NDHWC", "DHWIO", "NDHWC"),
        preferred_element_type=jnp.float32,
    )[0]


def pad_layer(field):
    return padded(field, (("space", 0),), 1)


def body(volume, weight_one, bias_one, weight_two, bias_two):
    slab_data = lax.all_to_all(volume, "space", split_axis=0, concat_axis=1, tiled=True)
    share = slab_data.shape[3]
    offset = lax.axis_index("chan") * share

    def layer(field, kernel, bias):
        part_kernel = lax.dynamic_slice_in_dim(kernel, offset, share, 3)
        summed = lax.psum_scatter(
            convolve(field, part_kernel), "chan", scatter_dimension=3, tiled=True
        )
        return summed + lax.dynamic_slice_in_dim(bias, offset, share, 0)

    hidden = jnp.maximum(layer(pad_layer(slab_data), weight_one, bias_one), 0.0).astype(
        jnp.bfloat16
    )
    result = layer(pad_layer(hidden), weight_two, bias_two)
    return jnp.maximum(result, 0.0).astype(jnp.bfloat16)


def solution(mesh):
    return jax.shard_map(
        body,
        mesh=mesh,
        in_specs=(P(None, "space", "tiles", "chan"), P(), P(), P(), P()),
        out_specs=P("space", None, "tiles", "chan"),
        check_vma=False,
    )
```

profile of v0, /device:TPU:0, one launch (start us, length us, event | category | flops | bytes accessed | tf_op | source)
XLA Modules:
  0.0 152.2 jit_solution(18392344283605213715)
XLA Ops:
  6.5 0.0 copy-start
  6.5 0.0 reduce-scatter.3.cloned.1.call-start
  6.5 33.3 %all_to_all.18 = bf16[32,8,16,128]{3,2,1,0:T(8,128)(2,1)S(1)} all-to-all(bf16[32,8,16,128]{3,2,1,0:T(8,128)(2,1)} %param.5), channel_id=1, replica_groups=mesh['tiles'=2,'space'=8,'chan'=2] {'space'}, dimensions={0} | all-to-all | bytes 2097152 | tf_op jit(solution)/shard_map/all_to_all | solution.py:36
  39.9 0.0 copy-start.2
  39.9 1.0 copy-done.2
  40.8 0.8 fusion.33
  41.7 4.1 %collective-permute-start = (bf16[1,64,16,128]{3,2,1,0:T(8,128)(2,1)}, bf16[1,64,16,128]{3,2,1,0:T(8,128)(2,1)}, u32[]{:S(2)}, u32[]{:S(2)}) collective-permute-start(bf16[1,64,16,128]{3,2,1,0:T(8,128)(2,1)} %bitcast.2), channel_id=1, source_target_pairs={{0,2},{2,4},{4,6},{6,8},{8,10},{10,12},{12,14},{1,3},{3,5},{5,7},{... | collective-permute-start | bytes 786440 | tf_op jit(solution)/shard_map/ppermute | solution.py:14
  45.7 1.3 collective-permute-start.1
  47.0 1.4 copy.14
  48.4 6.9 %collective-permute-done = bf16[1,64,16,128]{3,2,1,0:T(8,128)(2,1)} collective-permute-done((bf16[1,64,16,128]{3,2,1,0:T(8,128)(2,1)}, bf16[1,64,16,128]{3,2,1,0:T(8,128)(2,1)}, u32[]{:S(2)}, u32[]{:S(2)}) %collective-permute-start) | collective-permute-done | bytes 262176 | tf_op jit(solution)/shard_map/ppermute | solution.py:14
  55.4 0.0 collective-permute-done.1
  55.4 1.2 maximum_bitcast_fusion
  56.6 0.4 copy.23
  57.0 0.4 pad.clone
  57.4 1.5 %copy.17 = bf16[6,64,1,8,3,128]{5,3,4,1,0,2:T(8,128)(2,1)S(1)} copy(bf16[6,64,1,8,3,128]{5,1,4,3,0,2:T(8,128)(2,1)S(1)} %bitcast.31) | data formatting | bytes 4718592 | tf_op jit(solution)/shard_map/conv_general_dilated | solution.py:21
  58.9 0.0 copy-start.6
  58.9 0.4 slice.30
  59.4 0.0 copy-done
  59.4 0.2 copy-done.6
  59.6 13.5 %broadcast_select_fusion.1 = f32[4,64,8,3,256]{4,2,3,1,0:T(8,128)S(1)} fusion(pred[8,3]{0,1:T(4,128)(4,1)S(1)} %copy-done.6, bf16[6,64,1,7,2,128]{5,3,4,1,0,2:T(8,128)(2,1)S(1)} %slice.30, bf16[6,64,1,8,3,128]{5,3,4,1,0,2:T(8,128)(2,1)S(1)} %copy.17, bf16[3,3,3,256,256]{4,3,2,1,0:T(8,128)(2,1)S(1)} %copy-done, s32[]{:T(128)S(6)} %select_n.2), kind=kOutput, calls=%fused_computation.18 | convolution fusion | flops 10771759104 | bytes 11993604 | tf_op jit(solution)/shard_map/conv_general_dilated | solution.py:21
  73.0 1.9 %copy.18 = f32[4,64,8,3,256]{4,1,3,2,0:T(8,128)S(1)} copy(f32[4,64,8,3,256]{4,2,3,1,0:T(8,128)S(1)} %broadcast_select_fusion.1) | data formatting | bytes 12582912 | tf_op jit(solution)/shard_map/conv_general_dilated | solution.py:21
  75.0 2.4 %slice_bitcast_fusion.1 = f32[4,64,16,256]{3,1,2,0:T(8,128)} fusion(f32[4,64,1,24,256]{4,1,3,0,2:T(8,128)S(1)} %bitcast.28), kind=kLoop, calls=%fused_computation.4 | loop fusion | bytes 8388608 | tf_op jit(solution)/shard_map/squeeze | solution.py:21
  77.4 0.0 reduce-scatter.3.cloned.1.call-update
  77.4 0.0 reduce-scatter.5.cloned.1.call-start
  77.5 0.6 copy-done.4
  78.1 0.1 dynamic_slice.13
  78.2 11.9 %reduce-scatter.3.cloned.1.call-done = f32[4,64,16,128]{3,1,2,0:T(8,128)} async-done(((f32[4,64,16,256]{3,1,2,0:T(8,128)}), f32[4,64,16,128]{3,1,2,0:T(8,128)}) %reduce-scatter.3.cloned.1.call-update) | async-done | bytes 2097168 | tf_op jit(solution)/shard_map/reduce_scatter | solution.py:42
  90.1 1.9 %maximum_convert_fusion.1 = bf16[4,64,16,128]{3,1,2,0:T(8,128)(2,1)S(1)} fusion(f32[4,64,16,128]{3,1,2,0:T(8,128)} %reduce-scatter.3.cloned.1.call-done, f32[128]{0:T(128)S(1)} %dynamic_slice.13), kind=kLoop, calls=%fused_computation.20 | loop fusion | flops 1572864 | bytes 3146240 | tf_op jit(solution)/shard_map/convert_element_type | solution.py:47
  92.0 3.8 %collective-permute-start.2 = (bf16[1,64,16,128]{3,1,2,0:T(8,128)(2,1)S(1)}, bf16[1,64,16,128]{3,1,2,0:T(8,128)(2,1)S(1)}, u32[]{:S(2)}, u32[]{:S(2)}) collective-permute-start(bf16[1,64,16,128]{3,1,2,0:T(8,128)(2,1)S(1)} %get-tuple-element.5), channel_id=1, source_target_pairs={{0,2},{2,4},{4,6},{6,8},{8,10},{10,12},{12,14},{1,3},{3,5},{5,7},{... | collective-permute-start | bytes 786440 | tf_op jit(solution)/shard_map/ppermute | solution.py:14
  95.8 1.5 collective-permute-start.3
  97.2 10.0 %collective-permute-done.2 = bf16[1,64,16,128]{3,1,2,0:T(8,128)(2,1)S(1)} collective-permute-done((bf16[1,64,16,128]{3,1,2,0:T(8,128)(2,1)S(1)}, bf16[1,64,16,128]{3,1,2,0:T(8,128)(2,1)S(1)}, u32[]{:S(2)}, u32[]{:S(2)}) %collective-permute-start.2) | collective-permute-done | bytes 262176 | tf_op jit(solution)/shard_map/ppermute | solution.py:14
  107.3 0.0 collective-permute-done.3
  107.3 0.2 maximum_bitcast_fusion.1
  107.5 0.4 pad.2
  107.8 0.0 copy-start.3
  107.9 1.5 %copy.20 = bf16[6,64,1,8,3,128]{5,3,4,1,0,2:T(8,128)(2,1)S(1)} copy(bf16[6,64,1,8,3,128]{5,1,4,3,0,2:T(8,128)(2,1)S(1)} %bitcast.30) | data formatting | bytes 4718592 | tf_op jit(solution)/shard_map/conv_general_dilated | solution.py:21
  109.4 0.4 slice.34
  109.8 0.0 copy-done.3
  109.9 13.5 %broadcast_select_fusion = f32[4,64,8,3,256]{4,2,3,1,0:T(8,128)S(1)} fusion(pred[8,3]{0,1:T(4,128)(4,1)S(1)} %copy-done.6, bf16[6,64,1,7,2,128]{5,3,4,1,0,2:T(8,128)(2,1)S(1)} %slice.34, bf16[6,64,1,8,3,128]{5,3,4,1,0,2:T(8,128)(2,1)S(1)} %copy.20, bf16[3,3,3,256,256]{4,3,2,1,0:T(8,128)(2,1)S(1)} %copy-done.3, s32[]{:T(128)S(6)} %select_n.2), kind=kOutput, calls=%fused_computation.17 | convolution fusion | flops 10771759104 | bytes 11993604 | tf_op jit(solution)/shard_map/conv_general_dilated | solution.py:21
  123.3 1.9 %copy.21 = f32[4,64,8,3,256]{4,1,3,2,0:T(8,128)S(1)} copy(f32[4,64,8,3,256]{4,2,3,1,0:T(8,128)S(1)} %broadcast_select_fusion) | data formatting | bytes 12582912 | tf_op jit(solution)/shard_map/conv_general_dilated | solution.py:21
  125.3 2.4 %slice_bitcast_fusion = f32[4,64,16,256]{3,1,2,0:T(8,128)} fusion(f32[4,64,1,24,256]{4,1,3,0,2:T(8,128)S(1)} %bitcast.29), kind=kLoop, calls=%fused_computation.3 | loop fusion | bytes 8388608 | tf_op jit(solution)/shard_map/squeeze | solution.py:21
  127.7 0.0 reduce-scatter.5.cloned.1.call-update
  127.8 0.7 copy-done.5
  128.4 0.1 dynamic_slice.15
  128.5 13.4 %reduce-scatter.5.cloned.1.call-done = f32[4,64,16,128]{3,1,2,0:T(8,128)} async-done(((f32[4,64,16,256]{3,1,2,0:T(8,128)}), f32[4,64,16,128]{3,1,2,0:T(8,128)}) %reduce-scatter.5.cloned.1.call-update) | async-done | bytes 2097168 | tf_op jit(solution)/shard_map/reduce_scatter | solution.py:42
  141.8 1.9 %maximum_convert_fusion = bf16[4,64,16,128]{3,1,2,0:T(8,128)(2,1)S(1)} fusion(f32[4,64,16,128]{3,1,2,0:T(8,128)} %reduce-scatter.5.cloned.1.call-done, f32[128]{0:T(128)S(1)} %dynamic_slice.15), kind=kLoop, calls=%fused_computation.19 | loop fusion | flops 1572864 | bytes 3146240 | tf_op jit(solution)/shard_map/convert_element_type | solution.py:51
  143.7 1.7 %copy.22 = bf16[4,64,16,128]{3,2,1,0:T(8,128)(2,1)} copy(bf16[4,64,16,128]{3,1,2,0:T(8,128)(2,1)S(1)} %maximum_convert_fusion) | data formatting | bytes 2097152 | tf_op jit(solution)/shard_map/convert_element_type | solution.py:51
  145.4 0.0 copy-done.1
  (4 shorter events, 0.0 us)
Async XLA Ops:
  6.5 52.8 %copy-start = (bf16[3,3,3,256,256]{4,3,2,1,0:T(8,128)(2,1)S(1)}, bf16[3,3,3,256,256]{4,3,2,1,0:T(8,128)(2,1)}, u32[]{:S(2)}) copy-start(bf16[3,3,3,256,256]{4,3,2,1,0:T(8,128)(2,1)} %param.6) | copy-start | bytes 10616836
  6.5 83.5 %reduce-scatter.3.cloned.1.call-start = ((), (), s32[]{:S(2)}) async-start(), calls=%async_computation.3 | async-start | bytes 6291456 | tf_op jit(solution)/shard_map/reduce_scatter | solution.py:42
  39.9 1.0 copy-start.2
  41.7 13.7 %collective-permute-start = (bf16[1,64,16,128]{3,2,1,0:T(8,128)(2,1)}, bf16[1,64,16,128]{3,2,1,0:T(8,128)(2,1)}, u32[]{:S(2)}, u32[]{:S(2)}) collective-permute-start(bf16[1,64,16,128]{3,2,1,0:T(8,128)(2,1)} %bitcast.2), channel_id=1, source_target_pairs={{0,2},{2,4},{4,6},{6,8},{8,10},{10,12},{12,14},{1,3},{3,5},{5,7},{... | collective-permute-start | bytes 786440 | tf_op jit(solution)/shard_map/ppermute | solution.py:14
  45.7 9.6 %collective-permute-start.1 = (bf16[1,64,16,128]{3,2,1,0:T(8,128)(2,1)}, bf16[1,64,16,128]{3,2,1,0:T(8,128)(2,1)}, u32[]{:S(2)}, u32[]{:S(2)}) collective-permute-start(bf16[1,64,16,128]{3,2,1,0:T(8,128)(2,1)} %bitcast.5), channel_id=1, source_target_pairs={{2,0},{4,2},{6,4},{8,6},{10,8},{12,10},{14,12},{3,1},{5,3},{7,5},{... | collective-permute-start | bytes 786440 | tf_op jit(solution)/shard_map/ppermute | solution.py:15
  58.9 0.7 copy-start.6
  77.4 0.7 copy-start.4
  77.4 64.4 %reduce-scatter.5.cloned.1.call-start = ((), (), s32[]{:S(2)}) async-start(), calls=%async_computation.4 | async-start | bytes 6291456 | tf_op jit(solution)/shard_map/reduce_scatter | solution.py:42
  92.0 15.3 %collective-permute-start.2 = (bf16[1,64,16,128]{3,1,2,0:T(8,128)(2,1)S(1)}, bf16[1,64,16,128]{3,1,2,0:T(8,128)(2,1)S(1)}, u32[]{:S(2)}, u32[]{:S(2)}) collective-permute-start(bf16[1,64,16,128]{3,1,2,0:T(8,128)(2,1)S(1)} %get-tuple-element.5), channel_id=1, source_target_pairs={{0,2},{2,4},{4,6},{6,8},{8,10},{10,12},{12,14},{1,3},{3,5},{5,7},{... | collective-permute-start | bytes 786440 | tf_op jit(solution)/shard_map/ppermute | solution.py:14
  95.8 11.5 %collective-permute-start.3 = (bf16[1,64,16,128]{3,1,2,0:T(8,128)(2,1)S(1)}, bf16[1,64,16,128]{3,1,2,0:T(8,128)(2,1)S(1)}, u32[]{:S(2)}, u32[]{:S(2)}) collective-permute-start(bf16[1,64,16,128]{3,1,2,0:T(8,128)(2,1)S(1)} %get-tuple-element.6), channel_id=1, source_target_pairs={{2,0},{4,2},{6,4},{8,6},{10,8},{12,10},{14,12},{3,1},{5,3},{7,5},{... | collective-permute-start | bytes 786440 | tf_op jit(solution)/shard_map/ppermute | solution.py:15
  107.8 2.0 %copy-start.3 = (bf16[3,3,3,256,256]{4,3,2,1,0:T(8,128)(2,1)S(1)}, bf16[3,3,3,256,256]{4,3,2,1,0:T(8,128)(2,1)}, u32[]{:S(2)}) copy-start(bf16[3,3,3,256,256]{4,3,2,1,0:T(8,128)(2,1)} %param.8) | copy-start | bytes 10616836
  127.7 0.7 copy-start.5
  128.4 17.0 %copy-start.1 = (bf16[3,3,3,256,256]{4,3,2,1,0:T(8,128)(2,1)S(1)}, bf16[3,3,3,256,256]{4,3,2,1,0:T(8,128)(2,1)}, u32[]{:S(2)}) copy-start(bf16[3,3,3,256,256]{4,3,2,1,0:T(8,128)(2,1)} %param.6) | copy-start | bytes 10616836
Sparse Core Ops, SparseCore 0:
  77.6 12.4 reduce-scatter.2
  127.9 13.9 reduce-scatter.4
where the time goes:
time: 153 us; the launch traced here: 152 us
  waiting for transfers between devices  42.2 us (28%)
  blocking collectives  33.3 us (22%)
  matrix products  26.9 us (18%)
  local copies, waits for them, and re-layouts  20.4 us (13%)
  between operations  13.6 us (9%)
  starting transfers between devices  10.6 us (7%)
  other arithmetic  5.18 us (3%)
    all_to_all x1, blocking collectives, body(): lax.all_to_all(volume, 'space', split_axis=0, concat_axis=1, tiled=True)  33.3 us
    conv_general_dilated x2, matrix products, convolve(): lax.conv_general_dilated(field[None], kernel, (1, 1, 1), ((0, 0), (1, 1),...  26.9 us
    reduce_scatter x2, waiting for transfers between devices, layer(): lax.psum_scatter(convolve(field, part_kernel), 'chan', scatter_dimension=...  25.3 us
    ppermute x2, waiting for transfers between devices, padded(): before = lax.ppermute(last, axis, up)  17 us
    ppermute x2, starting transfers between devices, padded(): before = lax.ppermute(last, axis, up)  7.83 us
    conv_general_dilated x6, local copies, waits for them, and re-layouts, convolve(): lax.conv_general_dilated(field[None], kernel, (1, 1, 1), ((0, 0), (1, 1),...  7.73 us
    squeeze x2, local copies, waits for them, and re-layouts, convolve(): lax.conv_general_dilated(field[None], kernel, (1, 1, 1), ((0, 0), (1, 1),...  4.89 us
  transfers between devices with their start and end apart: 6, of which 4 were waited for; matrix products, arithmetic and copies ran while one was open for 1% of the time, Pallas kernels for 0%

commit v1 on v0

--- a/solution.py
+++ b/solution.py
@@ -2,6 +2,18 @@
 import jax.numpy as jnp
 from jax import lax
 from jax.sharding import PartitionSpec as P
+
+
+def split_up(shard, dim, count):
+    dims = shard.shape
+    tiles = shard.reshape(*dims[:dim], count, dims[dim] // count, *dims[dim + 1 :])
+    return jnp.moveaxis(tiles, dim, 0)
+
+
+def joined_along(tiles, dim):
+    tiles = jnp.moveaxis(tiles, 0, dim)
+    shape = tiles.shape
+    return tiles.reshape(*shape[:dim], shape[dim] * shape[dim + 1], *shape[dim + 2 :])
 
 
 def padded(x, sides, width):
@@ -33,7 +45,14 @@
 
 
 def body(volume, weight_one, bias_one, weight_two, bias_two):
-    slab_data = lax.all_to_all(volume, "space", split_axis=0, concat_axis=1, tiled=True)
+    size, index = (lax.axis_size("space"), lax.axis_index("space"))
+    tiles = split_up(volume, 0, size)
+    outs = [tiles[index]]
+    for turn in range(1, size):
+        sent = tiles[index ^ turn]
+        outs.append(lax.ppermute(sent, "space", [(i_2, i_2 ^ turn) for i_2 in range(size)]))
+    tiles = jnp.stack(outs)[index ^ jnp.arange(size)]
+    slab_data = joined_along(tiles, 1)
     share = slab_data.shape[3]
     offset = lax.axis_index("chan") * share
 

time: 153 us -> 157 us (1.026)
  blocking collectives: 33.3 us -> 0 us
  waiting for transfers between devices: 42.2 us -> 56.8 us
  starting transfers between devices: 10.6 us -> 23.8 us
  local copies, waits for them, and re-layouts: 20.4 us -> 30.4 us
    all_to_all x1 -> x0, blocking collectives: 33.3 us -> none  [body(): lax.all_to_all(volume, 'space', split_axis=0, concat_axis=1, tiled=True)]
    ppermute x0 -> x7, starting transfers between devices: none -> 13.1 us  [body(): lax.ppermute(sent, 'space', [(i_2, i_2 ^ turn) for i_2 in range(size)])]
    ppermute x2, waiting for transfers between devices: 0.01 us -> 12.1 us  [padded(): after = lax.ppermute(first, axis, down)]
    ppermute x0 -> x7, waiting for transfers between devices: none -> 11.2 us  [body(): lax.ppermute(sent, 'space', [(i_2, i_2 ^ turn) for i_2 in range(size)])]
    ppermute x2, waiting for transfers between devices: 17 us -> 6.52 us  [padded(): before = lax.ppermute(last, axis, up)]
    unnamed x15 -> x19, local copies, waits for them, and re-layouts: 2.91 us -> 5.93 us
    gather x0 -> x1, local copies, waits for them, and re-layouts: none -> 2.89 us  [body(): tiles = jnp.stack(outs)[index ^ jnp.arange(size)]]
    squeeze x0 -> x1, local copies, waits for them, and re-layouts: none -> 2.4 us  [body(): sent = tiles[index ^ turn]]
  transfers between devices with their start and end apart: 6 -> 13, of which waited for: 4 -> 8; matrix products, arithmetic and copies ran while one was open for 1% -> 4% of each run, Pallas kernels for 0% -> 0%
where the time goes in v1:
time: 157 us
  waiting for transfers between devices  56.8 us (36%)
  local copies, waits for them, and re-layouts  30.4 us (19%)
  matrix products  26.9 us (17%)
  starting transfers between devices  23.8 us (15%)
  between operations  13.6 us (9%)
  other arithmetic  5.19 us (3%)
    reduce_scatter x2, waiting for transfers between devices, layer(): lax.psum_scatter(convolve(field, part_kernel), 'chan', scatter_dimension=...  27.1 us
    conv_general_dilated x2, matrix products, convolve(): lax.conv_general_dilated(field[None], kernel, (1, 1, 1), ((0, 0), (1, 1),...  26.9 us
    ppermute x7, starting transfers between devices, body(): lax.ppermute(sent, 'space', [(i_2, i_2 ^ turn) for i_2 in range(size)])  13.1 us
    ppermute x2, waiting for transfers between devices, padded(): after = lax.ppermute(first, axis, down)  12.1 us
    ppermute x7, waiting for transfers between devices, body(): lax.ppermute(sent, 'space', [(i_2, i_2 ^ turn) for i_2 in range(size)])  11.2 us
    ppermute x2, starting transfers between devices, padded(): before = lax.ppermute(last, axis, up)  8.06 us
    conv_general_dilated x6, local copies, waits for them, and re-layouts, convolve(): lax.conv_general_dilated(field[None], kernel, (1, 1, 1), ((0, 0), (1, 1),...  7.73 us
    ppermute x2, waiting for transfers between devices, padded(): before = lax.ppermute(last, axis, up)  6.52 us
  transfers between devices with their start and end apart: 13, of which 8 were waited for; matrix products, arithmetic and copies ran while one was open for 4% of the time, Pallas kernels for 0%

profile of v1, /device:TPU:0, one launch (start us, length us, event | category | flops | bytes accessed | tf_op | source)
XLA Modules:
  0.0 156.8 jit_solution(14129470438218797391)
XLA Ops:
  6.5 2.4 %dynamic-slice_bitcast_fusion = (bf16[4,8,16,128]{3,2,1,0:T(8,128)(2,1)S(1)}, bf16[4,8,16,128]{3,2,1,0:T(8,128)(2,1)S(1)}, bf16[4,8,16,128]{3,2,1,0:T(8,128)(2,1...) fusion(bf16[8,4,8,16,128]{4,3,2,1,0:T(8,128)(2,1)} %bitcast.64,, ...), kind=kLoop, calls=%fused_computation.35 | loop fusion | bytes 2097184 | tf_op jit(solution)/shard_map/squeeze | solution.py:52
  8.9 3.0 %collective-permute-start = (bf16[4,8,16,128]{3,2,1,0:T(8,128)(2,1)S(1)}, bf16[4,8,16,128]{3,2,1,0:T(8,128)(2,1)S(1)}, u32[]{:S(2)}, u32[]{:S(2)}) collective-permute-start(bf16[4,8,16,128]{3,2,1,0:T(8,128)(2,1)S(1)} %get-tuple-element.15), channel_id=1, source_target_pairs={{0,2},{2,0},{4,6},{6,4},{8,10},{10,8},{12,14},{14,12},{1,3},{3,1},... | collective-permute-start | bytes 393224 | tf_op jit(solution)/shard_map/ppermute | solution.py:53
  11.9 1.6 %collective-permute-start.1 = (bf16[4,8,16,128]{3,2,1,0:T(8,128)(2,1)S(1)}, bf16[4,8,16,128]{3,2,1,0:T(8,128)(2,1)S(1)}, u32[]{:S(2)}, u32[]{:S(2)}) collective-permute-start(bf16[4,8,16,128]{3,2,1,0:T(8,128)(2,1)S(1)} %get-tuple-element.14), channel_id=1, source_target_pairs={{0,4},{2,6},{4,0},{6,2},{8,12},{10,14},{12,8},{14,10},{1,5},{3,7},... | collective-permute-start | bytes 393224 | tf_op jit(solution)/shard_map/ppermute | solution.py:53
  13.5 3.0 %collective-permute-start.3 = (bf16[4,8,16,128]{3,2,1,0:T(8,128)(2,1)S(1)}, bf16[4,8,16,128]{3,2,1,0:T(8,128)(2,1)S(1)}, u32[]{:S(2)}, u32[]{:S(2)}) collective-permute-start(bf16[4,8,16,128]{3,2,1,0:T(8,128)(2,1)S(1)} %get-tuple-element.12), channel_id=1, source_target_pairs={{0,8},{2,10},{4,12},{6,14},{8,0},{10,2},{12,4},{14,6},{1,9},{3,11}... | collective-permute-start | bytes 393224 | tf_op jit(solution)/shard_map/ppermute | solution.py:53
  16.5 1.3 collective-permute-start.4
  17.8 3.7 %collective-permute-start.5 = (bf16[4,8,16,128]{3,2,1,0:T(8,128)(2,1)S(1)}, bf16[4,8,16,128]{3,2,1,0:T(8,128)(2,1)S(1)}, u32[]{:S(2)}, u32[]{:S(2)}) collective-permute-start(bf16[4,8,16,128]{3,2,1,0:T(8,128)(2,1)S(1)} %get-tuple-element.10), channel_id=1, source_target_pairs={{0,12},{2,14},{4,8},{6,10},{8,4},{10,6},{12,0},{14,2},{1,13},{3,15... | collective-permute-start | bytes 393224 | tf_op jit(solution)/shard_map/ppermute | solution.py:53
  21.4 0.7 bitcast_dynamic-update-slice_fusion.6
  22.1 0.5 collective-permute-done.1
  22.6 0.7 collective-permute-start.6
  23.3 0.7 bitcast_dynamic-update-slice_fusion.5
  24.0 0.7 bitcast_dynamic-update-slice_fusion.4
  24.6 0.7 bitcast_dynamic-update-slice_fusion.3
  25.3 10.6 %collective-permute-done.4 = bf16[4,8,16,128]{3,2,1,0:T(8,128)(2,1)S(1)} collective-permute-done((bf16[4,8,16,128]{3,2,1,0:T(8,128)(2,1)S(1)}, bf16[4,8,16,128]{3,2,1,0:T(8,128)(2,1)S(1)}, u32[]{:S(2)}, u32[]{:S(2)}) %collective-permute-start.4) | collective-permute-done | bytes 131104 | tf_op jit(solution)/shard_map/ppermute | solution.py:53
  35.9 0.7 bitcast_dynamic-update-slice_fusion.2
  36.6 0.7 bitcast_dynamic-update-slice_fusion.1
  37.2 0.7 bitcast_dynamic-update-slice_fusion
  37.9 2.9 %gather_fusion = bf16[8,4,8,16,128]{4,3,2,1,0:T(8,128)(2,1)} fusion(bf16[8,4,8,16,128]{4,3,2,1,0:T(8,128)(2,1)} %bitcast_dynamic-update-slice_fusion, s32[1024]{0:T(1024)S(1)} %pad_clamp_fusion), kind=kCustom, calls=%fused_computation | custom fusion | bytes 2097184 | tf_op jit(solution)/shard_map/gather | solution.py:54
  40.8 1.9 %fusion.34 = (bf16[1,8,8,16,128]{4,3,2,0,1:T(8,128)(2,1)}, bf16[1,8,8,16,128]{4,3,2,0,1:T(8,128)(2,1)}) fusion(bf16[4,8,8,16,128]{4,3,2,0,1:T(8,128)(2,1)} %bitcast.61), kind=kLoop, calls=%fused_computation.55 | loop fusion | bytes 1048576 | tf_op jit(solution)/shard_map/slice | solution.py:24
  42.7 3.3 %collective-permute-start.7 = (bf16[1,64,16,128]{3,2,1,0:T(8,128)(2,1)}, bf16[1,64,16,128]{3,2,1,0:T(8,128)(2,1)}, u32[]{:S(2)}, u32[]{:S(2)}) collective-permute-start(bf16[1,64,16,128]{3,2,1,0:T(8,128)(2,1)} %bitcast.17), channel_id=1, source_target_pairs={{0,2},{2,4},{4,6},{6,8},{8,10},{10,12},{12,14},{1,3},{3,5},{5,7},{... | collective-permute-start | bytes 786440 | tf_op jit(solution)/shard_map/ppermute | solution.py:26
  46.0 1.3 collective-permute-start.8
  47.3 1.4 copy.14
  48.7 0.8 collective-permute-done.7
  49.5 7.7 %collective-permute-done.8 = bf16[1,64,16,128]{3,2,1,0:T(8,128)(2,1)} collective-permute-done((bf16[1,64,16,128]{3,2,1,0:T(8,128)(2,1)}, bf16[1,64,16,128]{3,2,1,0:T(8,128)(2,1)}, u32[]{:S(2)}, u32[]{:S(2)}) %collective-permute-start.8) | collective-permute-done | bytes 262176 | tf_op jit(solution)/shard_map/ppermute | solution.py:27
  57.2 1.2 maximum_bitcast_fusion
  58.4 0.4 copy.23
  58.8 0.4 pad.clone
  59.2 1.5 copy.17
  60.7 0.4 slice.32
  61.4 13.5 %broadcast_select_fusion.1 = f32[4,64,8,3,256]{4,2,3,1,0:T(8,128)S(1)} fusion(pred[8,3]{0,1:T(4,128)(4,1)S(1)} %copy-done.5, bf16[6,64,1,7,2,128]{5,3,4,1,0,2:T(8,128)(2,1)S(1)} %slice.32, bf16[6,64,1,8,3,128]{5,3,4,1,0,2:T(8,128)(2,1)S(1)} %copy.17, bf16[3,3,3,256,256]{4,3,2,1,0:T(8,128)(2,1)S(1)} %copy-done, s32[]{:T(128)S(6)} %select_n.49), kind=kOutput, calls=%fused_computation.19 | convolution fusion | flops 10771759104 | bytes 11993604 | tf_op jit(solution)/shard_map/conv_general_dilated | solution.py:33
  74.9 1.9 %copy.18 = f32[4,64,8,3,256]{4,1,3,2,0:T(8,128)S(1)} copy(f32[4,64,8,3,256]{4,2,3,1,0:T(8,128)S(1)} %broadcast_select_fusion.1) | data formatting | bytes 12582912 | tf_op jit(solution)/shard_map/conv_general_dilated | solution.py:33
  76.8 2.4 %slice_bitcast_fusion.1 = f32[4,64,16,256]{3,1,2,0:T(8,128)} fusion(f32[4,64,1,24,256]{4,1,3,0,2:T(8,128)S(1)} %bitcast.57), kind=kLoop, calls=%fused_computation.5 | loop fusion | bytes 8388608 | tf_op jit(solution)/shard_map/squeeze | solution.py:33
  79.3 0.6 copy-done.3
  80.0 14.6 %reduce-scatter.3.cloned.1.call-done = f32[4,64,16,128]{3,1,2,0:T(8,128)} async-done(((f32[4,64,16,256]{3,1,2,0:T(8,128)}), f32[4,64,16,128]{3,1,2,0:T(8,128)}) %reduce-scatter.3.cloned.1.call-update) | async-done | bytes 2097168 | tf_op jit(solution)/shard_map/reduce_scatter | solution.py:61
  94.6 1.9 %maximum_convert_fusion.1 = bf16[4,64,16,128]{3,1,2,0:T(8,128)(2,1)S(1)} fusion(f32[4,64,16,128]{3,1,2,0:T(8,128)} %reduce-scatter.3.cloned.1.call-done, f32[128]{0:T(128)S(1)} %dynamic_slice.45), kind=kLoop, calls=%fused_computation.21 | loop fusion | flops 1572864 | bytes 3146240 | tf_op jit(solution)/shard_map/convert_element_type | solution.py:66
  96.5 1.3 collective-permute-start.10
  97.8 4.7 %collective-permute-start.9 = (bf16[1,64,16,128]{3,1,2,0:T(8,128)(2,1)S(1)}, bf16[1,64,16,128]{3,1,2,0:T(8,128)(2,1)S(1)}, u32[]{:S(2)}, u32[]{:S(2)}) collective-permute-start(bf16[1,64,16,128]{3,1,2,0:T(8,128)(2,1)S(1)} %get-tuple-element.5), channel_id=1, source_target_pairs={{0,2},{2,4},{4,6},{6,8},{8,10},{10,12},{12,14},{1,3},{3,5},{5,7},{... | collective-permute-start | bytes 786440 | tf_op jit(solution)/shard_map/ppermute | solution.py:26
  102.6 4.4 %collective-permute-done.10 = bf16[1,64,16,128]{3,1,2,0:T(8,128)(2,1)S(1)} collective-permute-done((bf16[1,64,16,128]{3,1,2,0:T(8,128)(2,1)S(1)}, bf16[1,64,16,128]{3,1,2,0:T(8,128)(2,1)S(1)}, u32[]{:S(2)}, u32[]{:S(2)}) %collective-permute-start.10) | collective-permute-done | bytes 262176 | tf_op jit(solution)/shard_map/ppermute | solution.py:27
  107.0 5.7 %collective-permute-done.9 = bf16[1,64,16,128]{3,1,2,0:T(8,128)(2,1)S(1)} collective-permute-done((bf16[1,64,16,128]{3,1,2,0:T(8,128)(2,1)S(1)}, bf16[1,64,16,128]{3,1,2,0:T(8,128)(2,1)S(1)}, u32[]{:S(2)}, u32[]{:S(2)}) %collective-permute-start.9) | collective-permute-done | bytes 262176 | tf_op jit(solution)/shard_map/ppermute | solution.py:26
  112.9 0.4 pad.2
  113.3 1.5 copy.20
  114.8 0.4 slice.36
  115.3 13.5 %broadcast_select_fusion = f32[4,64,8,3,256]{4,2,3,1,0:T(8,128)S(1)} fusion(pred[8,3]{0,1:T(4,128)(4,1)S(1)} %copy-done.5, bf16[6,64,1,7,2,128]{5,3,4,1,0,2:T(8,128)(2,1)S(1)} %slice.36, bf16[6,64,1,8,3,128]{5,3,4,1,0,2:T(8,128)(2,1)S(1)} %copy.20, bf16[3,3,3,256,256]{4,3,2,1,0:T(8,128)(2,1)S(1)} %copy-done.2, s32[]{:T(128)S(6)} %select_n.49), kind=kOutput, calls=%fused_computation.18 | convolution fusion | flops 10771759104 | bytes 11993604 | tf_op jit(solution)/shard_map/conv_general_dilated | solution.py:33
  128.8 1.9 %copy.21 = f32[4,64,8,3,256]{4,1,3,2,0:T(8,128)S(1)} copy(f32[4,64,8,3,256]{4,2,3,1,0:T(8,128)S(1)} %broadcast_select_fusion) | data formatting | bytes 12582912 | tf_op jit(solution)/shard_map/conv_general_dilated | solution.py:33
  130.7 2.4 %slice_bitcast_fusion = f32[4,64,16,256]{3,1,2,0:T(8,128)} fusion(f32[4,64,1,24,256]{4,1,3,0,2:T(8,128)S(1)} %bitcast.58), kind=kLoop, calls=%fused_computation.4 | loop fusion | bytes 8388608 | tf_op jit(solution)/shard_map/squeeze | solution.py:33
  133.2 0.7 copy-done.4
  133.9 12.5 %reduce-scatter.5.cloned.1.call-done = f32[4,64,16,128]{3,1,2,0:T(8,128)} async-done(((f32[4,64,16,256]{3,1,2,0:T(8,128)}), f32[4,64,16,128]{3,1,2,0:T(8,128)}) %reduce-scatter.5.cloned.1.call-update) | async-done | bytes 2097168 | tf_op jit(solution)/shard_map/reduce_scatter | solution.py:61
  146.4 1.9 %maximum_convert_fusion = bf16[4,64,16,128]{3,1,2,0:T(8,128)(2,1)S(1)} fusion(f32[4,64,16,128]{3,1,2,0:T(8,128)} %reduce-scatter.5.cloned.1.call-done, f32[128]{0:T(128)S(1)} %dynamic_slice.47), kind=kLoop, calls=%fused_computation.20 | loop fusion | flops 1572864 | bytes 3146240 | tf_op jit(solution)/shard_map/convert_element_type | solution.py:70
  148.3 1.7 %copy.22 = bf16[4,64,16,128]{3,2,1,0:T(8,128)(2,1)} copy(bf16[4,64,16,128]{3,1,2,0:T(8,128)(2,1)S(1)} %maximum_convert_fusion) | data formatting | bytes 2097152 | tf_op jit(solution)/shard_map/convert_element_type | solution.py:70
  (26 shorter events, 0.8 us)
Async XLA Ops:
  6.5 54.6 %copy-start = (bf16[3,3,3,256,256]{4,3,2,1,0:T(8,128)(2,1)S(1)}, bf16[3,3,3,256,256]{4,3,2,1,0:T(8,128)(2,1)}, u32[]{:S(2)}) copy-start(bf16[3,3,3,256,256]{4,3,2,1,0:T(8,128)(2,1)} %param.6) | copy-start | bytes 10616836
  6.5 88.1 %reduce-scatter.3.cloned.1.call-start = ((), (), s32[]{:S(2)}) async-start(), calls=%async_computation.2 | async-start | bytes 6291456 | tf_op jit(solution)/shard_map/reduce_scatter | solution.py:61
  8.9 8.8 %collective-permute-start = (bf16[4,8,16,128]{3,2,1,0:T(8,128)(2,1)S(1)}, bf16[4,8,16,128]{3,2,1,0:T(8,128)(2,1)S(1)}, u32[]{:S(2)}, u32[]{:S(2)}) collective-permute-start(bf16[4,8,16,128]{3,2,1,0:T(8,128)(2,1)S(1)} %get-tuple-element.15), channel_id=1, source_target_pairs={{0,2},{2,0},{4,6},{6,4},{8,10},{10,8},{12,14},{14,12},{1,3},{3,1},... | collective-permute-start | bytes 393224 | tf_op jit(solution)/shard_map/ppermute | solution.py:53
  11.9 10.7 %collective-permute-start.1 = (bf16[4,8,16,128]{3,2,1,0:T(8,128)(2,1)S(1)}, bf16[4,8,16,128]{3,2,1,0:T(8,128)(2,1)S(1)}, u32[]{:S(2)}, u32[]{:S(2)}) collective-permute-start(bf16[4,8,16,128]{3,2,1,0:T(8,128)(2,1)S(1)} %get-tuple-element.14), channel_id=1, source_target_pairs={{0,4},{2,6},{4,0},{6,2},{8,12},{10,14},{12,8},{14,10},{1,5},{3,7},... | collective-permute-start | bytes 393224 | tf_op jit(solution)/shard_map/ppermute | solution.py:53
  13.5 10.5 %collective-permute-start.2 = (bf16[4,8,16,128]{3,2,1,0:T(8,128)(2,1)S(1)}, bf16[4,8,16,128]{3,2,1,0:T(8,128)(2,1)S(1)}, u32[]{:S(2)}, u32[]{:S(2)}) collective-permute-start(bf16[4,8,16,128]{3,2,1,0:T(8,128)(2,1)S(1)} %get-tuple-element.13), channel_id=1, source_target_pairs={{0,6},{2,4},{4,2},{6,0},{8,14},{10,12},{12,10},{14,8},{1,7},{3,5},... | collective-permute-start | bytes 393224 | tf_op jit(solution)/shard_map/ppermute | solution.py:53
  13.5 11.1 %collective-permute-start.3 = (bf16[4,8,16,128]{3,2,1,0:T(8,128)(2,1)S(1)}, bf16[4,8,16,128]{3,2,1,0:T(8,128)(2,1)S(1)}, u32[]{:S(2)}, u32[]{:S(2)}) collective-permute-start(bf16[4,8,16,128]{3,2,1,0:T(8,128)(2,1)S(1)} %get-tuple-element.12), channel_id=1, source_target_pairs={{0,8},{2,10},{4,12},{6,14},{8,0},{10,2},{12,4},{14,6},{1,9},{3,11}... | collective-permute-start | bytes 393224 | tf_op jit(solution)/shard_map/ppermute | solution.py:53
  16.5 19.5 %collective-permute-start.4 = (bf16[4,8,16,128]{3,2,1,0:T(8,128)(2,1)S(1)}, bf16[4,8,16,128]{3,2,1,0:T(8,128)(2,1)S(1)}, u32[]{:S(2)}, u32[]{:S(2)}) collective-permute-start(bf16[4,8,16,128]{3,2,1,0:T(8,128)(2,1)S(1)} %get-tuple-element.11), channel_id=1, source_target_pairs={{0,10},{2,8},{4,14},{6,12},{8,2},{10,0},{12,6},{14,4},{1,11},{3,9}... | collective-permute-start | bytes 393224 | tf_op jit(solution)/shard_map/ppermute | solution.py:53
  17.8 18.8 %collective-permute-start.5 = (bf16[4,8,16,128]{3,2,1,0:T(8,128)(2,1)S(1)}, bf16[4,8,16,128]{3,2,1,0:T(8,128)(2,1)S(1)}, u32[]{:S(2)}, u32[]{:S(2)}) collective-permute-start(bf16[4,8,16,128]{3,2,1,0:T(8,128)(2,1)S(1)} %get-tuple-element.10), channel_id=1, source_target_pairs={{0,12},{2,14},{4,8},{6,10},{8,4},{10,6},{12,0},{14,2},{1,13},{3,15... | collective-permute-start | bytes 393224 | tf_op jit(solution)/shard_map/ppermute | solution.py:53
  22.6 14.6 %collective-permute-start.6 = (bf16[4,8,16,128]{3,2,1,0:T(8,128)(2,1)S(1)}, bf16[4,8,16,128]{3,2,1,0:T(8,128)(2,1)S(1)}, u32[]{:S(2)}, u32[]{:S(2)}) collective-permute-start(bf16[4,8,16,128]{3,2,1,0:T(8,128)(2,1)S(1)} %get-tuple-element.9), channel_id=1, source_target_pairs={{0,14},{2,12},{4,10},{6,8},{8,6},{10,4},{12,2},{14,0},{1,15},{3,13... | collective-permute-start | bytes 393224 | tf_op jit(solution)/shard_map/ppermute | solution.py:53
  42.7 6.8 %collective-permute-start.7 = (bf16[1,64,16,128]{3,2,1,0:T(8,128)(2,1)}, bf16[1,64,16,128]{3,2,1,0:T(8,128)(2,1)}, u32[]{:S(2)}, u32[]{:S(2)}) collective-permute-start(bf16[1,64,16,128]{3,2,1,0:T(8,128)(2,1)} %bitcast.17), channel_id=1, source_target_pairs={{0,2},{2,4},{4,6},{6,8},{8,10},{10,12},{12,14},{1,3},{3,5},{5,7},{... | collective-permute-start | bytes 786440 | tf_op jit(solution)/shard_map/ppermute | solution.py:26
  46.0 11.2 %collective-permute-start.8 = (bf16[1,64,16,128]{3,2,1,0:T(8,128)(2,1)}, bf16[1,64,16,128]{3,2,1,0:T(8,128)(2,1)}, u32[]{:S(2)}, u32[]{:S(2)}) collective-permute-start(bf16[1,64,16,128]{3,2,1,0:T(8,128)(2,1)} %bitcast.19), channel_id=1, source_target_pairs={{2,0},{4,2},{6,4},{8,6},{10,8},{12,10},{14,12},{3,1},{5,3},{7,5},{... | collective-permute-start | bytes 786440 | tf_op jit(solution)/shard_map/ppermute | solution.py:27
  60.7 0.7 copy-start.5
  79.2 0.7 copy-start.3
  79.3 67.1 %reduce-scatter.5.cloned.1.call-start = ((), (), s32[]{:S(2)}) async-start(), calls=%async_computation.3 | async-start | bytes 6291456 | tf_op jit(solution)/shard_map/reduce_scatter | solution.py:61
  96.5 10.4 %collective-permute-start.10 = (bf16[1,64,16,128]{3,1,2,0:T(8,128)(2,1)S(1)}, bf16[1,64,16,128]{3,1,2,0:T(8,128)(2,1)S(1)}, u32[]{:S(2)}, u32[]{:S(2)}) collective-permute-start(bf16[1,64,16,128]{3,1,2,0:T(8,128)(2,1)S(1)} %get-tuple-element.6), channel_id=1, source_target_pairs={{2,0},{4,2},{6,4},{8,6},{10,8},{12,10},{14,12},{3,1},{5,3},{7,5},{... | collective-permute-start | bytes 786440 | tf_op jit(solution)/shard_map/ppermute | solution.py:27
  97.8 14.9 %collective-permute-start.9 = (bf16[1,64,16,128]{3,1,2,0:T(8,128)(2,1)S(1)}, bf16[1,64,16,128]{3,1,2,0:T(8,128)(2,1)S(1)}, u32[]{:S(2)}, u32[]{:S(2)}) collective-permute-start(bf16[1,64,16,128]{3,1,2,0:T(8,128)(2,1)S(1)} %get-tuple-element.5), channel_id=1, source_target_pairs={{0,2},{2,4},{4,6},{6,8},{8,10},{10,12},{12,14},{1,3},{3,5},{5,7},{... | collective-permute-start | bytes 786440 | tf_op jit(solution)/shard_map/ppermute | solution.py:26
  113.3 2.0 %copy-start.2 = (bf16[3,3,3,256,256]{4,3,2,1,0:T(8,128)(2,1)S(1)}, bf16[3,3,3,256,256]{4,3,2,1,0:T(8,128)(2,1)}, u32[]{:S(2)}) copy-start(bf16[3,3,3,256,256]{4,3,2,1,0:T(8,128)(2,1)} %param.8) | copy-start | bytes 10616836
  133.2 0.7 copy-start.4
  133.8 16.1 %copy-start.1 = (bf16[3,3,3,256,256]{4,3,2,1,0:T(8,128)(2,1)S(1)}, bf16[3,3,3,256,256]{4,3,2,1,0:T(8,128)(2,1)}, u32[]{:S(2)}) copy-start(bf16[3,3,3,256,256]{4,3,2,1,0:T(8,128)(2,1)} %param.6) | copy-start | bytes 10616836
Sparse Core Ops, SparseCore 0:
  79.4 15.1 reduce-scatter.2
  133.3 13.0 reduce-scatter.4
